TPU v7x, 256 devices: a whole 4x4x8 slice. The times are simulated.
256 devices in a mesh: pole: 4 (over y), row: 8 (over z_lo, x), col: 8 (over z_hi, core).
Axes of the slice: x: 4, y: 4, z: 8 (z_hi: 4, z_lo: 2; z = z_hi * 2 + z_lo), core: 2. Of those that a mesh axis runs over, the one named last changes fastest.
Arguments:
- found_inverse: bfloat16 [4, 2, 8192, 8, 8, 128], P('pole', None, 'row', None, 'col'), may hold values from -0.125 to 0.125
- l_panel: bfloat16 [4, 2, 8192, 512], P('pole', None, ('row', 'col')), may hold values from -1.5 to 1.5
- block_pattern: int32 [64, 4], P(('row', 'col')), may hold values 0 or 1
- sup_widths: int32 [4], replicated, may hold values from 1 to 128, 320 in all
- diag_inverse: bfloat16 [4, 2, 512, 128], P('pole'), may hold values from -6 to 6
- pole_weights: float32 [4, 2], P('pole'), may hold values from -4 to 4
Outputs:
- density: float32 [512, 8192], P('col', 'row')
- diagonal: float32 [512, 128], replicated
Inputs may be any that keep to these rules, and one draw needn't show every extreme that they name: `sup_widths`: one supernode has exactly 128 columns.
All inputs are finite; a program needn't handle non-finite values. No bound on the sum of `block_pattern` on one device may be relied on, other than what follows from the above.
Results may differ from a plain program's by a relative error of at most 0.0003.
Values may be sent and summed in bfloat16 or wider, within the bound.
A program may use at most 128 MiB of HBM per device.

v0:
```python
import jax
import jax.numpy as jnp
from jax import lax
from jax.sharding import PartitionSpec as P


def contract(left, right):
    return jnp.einsum("jk,ij->ki", left, right, preferred_element_type=jnp.float32)


def pair_product(left, right):
    return jnp.einsum("ika,kbi->kab", left, right, precision=lax.Precision.HIGHEST)


def per_device(found_inverse, l_panel, block_pattern, sup_widths, diag_inverse, pole_weights):
    slot_width = diag_inverse.shape[-1]
    total_cols = l_panel.shape[-1]
    supernodes = total_cols // slot_width
    row_count = lax.axis_size("row")
    col_count = lax.axis_size("col")
    row_index = lax.axis_index("row")
    col_index = lax.axis_index("col")
    columns = jnp.arange(total_cols, dtype=jnp.int32)
    column_ok = columns % slot_width < jnp.repeat(sup_widths, slot_width)
    block_ok = jnp.repeat(block_pattern[0], slot_width) == 1
    masked = jnp.where(
        (column_ok & block_ok)[None, None, :], l_panel[0], jnp.zeros((), jnp.bfloat16)
    )
    everything = lax.all_gather(masked, ("row", "col"), axis=1, tiled=True)
    own_rows = lax.dynamic_slice_in_dim(
        everything, row_index * col_count * slot_width, col_count * slot_width, 1
    )
    grouped = everything.reshape(2, row_count, col_count, slot_width, total_cols)
    picked = lax.dynamic_index_in_dim(grouped, col_index, 2, keepdims=False)
    column_rows = picked.reshape(2, row_count * slot_width, total_cols)
    local_rows = found_inverse.shape[2]
    inverse = found_inverse[0].reshape(2, local_rows, row_count * slot_width)
    part_real = contract(column_rows[1], inverse[1]) - contract(column_rows[0], inverse[0])
    part_imag = -(contract(column_rows[1], inverse[0]) + contract(column_rows[0], inverse[1]))
    w_real = pole_weights[0, 0]
    w_imag = pole_weights[0, 1]
    weighted = w_real * part_real - w_imag * part_imag
    whole = lax.psum(weighted, "pole")
    density = lax.psum_scatter(whole, "col", scatter_dimension=0, tiled=True)
    lifted = own_rows.astype(jnp.float32).reshape(2, local_rows, supernodes, slot_width)
    upper_real = part_real.reshape(supernodes, slot_width, local_rows)
    upper_imag = part_imag.reshape(supernodes, slot_width, local_rows)
    t_real = pair_product(lifted[0], upper_real) - pair_product(lifted[1], upper_imag)
    t_imag = pair_product(lifted[0], upper_imag) + pair_product(lifted[1], upper_real)
    lead_flag = ((row_index == 0) & (col_index == 0)).astype(jnp.float32)
    d_real = diag_inverse[0, 0].astype(jnp.float32).reshape(supernodes, slot_width, slot_width)
    d_imag = diag_inverse[0, 1].astype(jnp.float32).reshape(supernodes, slot_width, slot_width)
    local_term = lead_flag * (w_real * d_real - w_imag * d_imag) - (
        w_real * t_real - w_imag * t_imag
    )
    diagonal = lax.psum(local_term.reshape(total_cols, slot_width), ("pole", "row", "col"))
    return (density, diagonal)


def solution(mesh):
    in_specs = (
        P("pole", None, "row", None, "col", None),
        P("pole", None, ("row", "col"), None),
        P(("row", "col"), None),
        P(),
        P("pole", None, None, None),
        P("pole", None),
    )
    out_specs = (P("col", "row"), P())
    return jax.shard_map(
        per_device, mesh=mesh, in_specs=in_specs, out_specs=out_specs, check_vma=False
    )
```

profile of v0, /device:TPU:2, one launch (start us, length us, event | category | flops | bytes accessed | tf_op | source)
XLA Modules:
  0.0 514.2 jit_solution(14721515015720495059)
XLA Ops:
  7.9 0.7 fusion.25
  8.6 1.7 bitcast_select_fusion
  10.4 1.3 fusion.27
  11.7 3.8 fusion.26
  15.5 127.3 %all-gather.2.cloned.1.call-done = bf16[2,8192,512]{2,1,0:T(8,128)(2,1)} async-done(((bf16[2,128,512]{2,1,0:T(8,128)(2,1)}), bf16[2,8192,512]{2,1,0:T(8,128)(2,1)}) %all-gather.2.cloned.1.call-update) | async-done | bytes 16777232 | tf_op jit(solution)/shard_map/all_gather | solution.py:29
  142.8 1.7 constant_dynamic-slice_fusion.3
  144.6 1.3 fusion
  145.9 1.3 fusion.2
  147.5 1.3 fusion.12
  148.8 4.6 multiply_subtract_fusion
  153.4 0.9 copy-done.3
  154.3 1.3 subtract_multiply_fusion
  155.6 3.0 constant_dynamic-slice_fusion.2
  158.6 1.5 copy.9
  160.1 2.3 copy.8
  162.3 3.3 fusion.29
  165.7 1.2 fusion.28
  167.3 1.9 fusion.20
  169.1 2.5 fusion.19
  171.7 25.0 %reduce-scatter.2.cloned.1.call-done = f32[64,1024]{1,0:T(8,128)} async-done(((f32[512,1024]{1,0:T(8,128)}), f32[64,1024]{1,0:T(8,128)}) %reduce-scatter.2.cloned.1.call-update) | async-done | bytes 262160 | tf_op jit(solution)/shard_map/reduce_scatter | solution.py:44
  196.7 259.6 %all-reduce.3.cloned.1.call-done = f32[512,128]{1,0:T(8,128)} async-done(((f32[512,128]{1,0:T(8,128)}), f32[512,128]{1,0:T(8,128)}) %all-reduce.3.cloned.1.call-update) | async-done | bytes 262160 | tf_op jit(solution)/shard_map/psum | solution.py:56
  456.3 48.0 %all-reduce.5.cloned.1.call-done = f32[64,1024]{1,0:T(8,128)} async-done(((f32[64,1024]{1,0:T(8,128)}), f32[64,1024]{1,0:T(8,128)}) %all-reduce.5.cloned.1.call-update) | async-done | bytes 262160 | tf_op jit(solution)/shard_map/psum | solution.py:43
  504.3 1.7 copy.36
  506.0 1.7 copy.37
  (16 shorter events, 1.5 us)
Async XLA Ops:
  7.2 135.7 %all-gather.2.cloned.1.call-start = ((), (), s32[]{:S(2)}) async-start(), calls=%async_computation.1 | async-start | bytes 17039360 | tf_op jit(solution)/shard_map/all_gather | solution.py:29
  10.3 186.4 %reduce-scatter.2.cloned.1.call-start = ((), (), s32[]{:S(2)}) async-start(), calls=%async_computation.3 | async-start | bytes 2359296 | tf_op jit(solution)/shard_map/reduce_scatter | solution.py:44
  145.9 1.6 copy-start.2
  153.4 0.9 copy-start.3
  153.4 302.9 %all-reduce.3.cloned.1.call-start = ((), (), s32[]{:S(2)}) async-start(), calls=%async_computation.2 | async-start | bytes 524288 | tf_op jit(solution)/shard_map/psum | solution.py:56
  162.3 3.3 copy-start.1
  165.7 1.6 copy-start
  171.6 332.7 %all-reduce.5.cloned.1.call-start = ((), (), s32[]{:S(2)}) async-start(), calls=%async_computation.4 | async-start | bytes 524288 | tf_op jit(solution)/shard_map/psum | solution.py:43
Sparse Core Ops, SparseCore 0:
  10.4 132.3 all-gather.1
  153.5 43.1 reduce-scatter.1
  202.7 253.5 all-reduce.2
  458.5 45.7 all-reduce.4
where the time goes:
time: 515 us; the launch traced here: 514 us
  waiting for transfers between devices  460 us (89%)
  local copies, waits for them, and re-layouts  18.5 us (4%)
  matrix products  17.3 us (3%)
  between operations  13.9 us (3%)
    psum x1, waiting for transfers between devices, per_device(): lax.psum(local_term.reshape(total_cols, slot_width), ('pole', 'row', 'col'))  260 us
    all_gather x1, waiting for transfers between devices, per_device(): everything = lax.all_gather(masked, ('row', 'col'), axis=1, tiled=True)  127 us
    psum x1, waiting for transfers between devices, per_device(): whole = lax.psum(weighted, 'pole')  48 us
    reduce_scatter x1, waiting for transfers between devices, per_device(): density = lax.psum_scatter(whole, 'col', scatter_dimension=0, tiled=True)  25 us
  transfers between devices with their start and end apart: 4, of which 4 were waited for; matrix products, arithmetic and copies ran while one was open for 4% of the time, Pallas kernels for 0%

commit v1 on v0

--- a/solution.py
+++ b/solution.py
@@ -53,7 +53,9 @@
     local_term = lead_flag * (w_real * d_real - w_imag * d_imag) - (
         w_real * t_real - w_imag * t_imag
     )
-    diagonal = lax.psum(local_term.reshape(total_cols, slot_width), ("pole", "row", "col"))
+    diagonal = local_term.reshape(total_cols, slot_width)
+    for axis in ("pole", ("row", "col")):
+        diagonal = lax.psum(diagonal, axis)
     return (density, diagonal)
 
 

time: 515 us -> 440 us (0.85)
  waiting for transfers between devices: 460 us -> 383 us
    psum x1, waiting for transfers between devices: 260 us -> 180 us  [per_device(): diagonal = lax.psum(diagonal, axis)]
  transfers between devices with their start and end apart: 4 -> 4, of which waited for: 4 -> 4; matrix products, arithmetic and copies ran while one was open for 4% -> 5% of each run, Pallas kernels for 0% -> 0%
where the time goes in v1:
time: 440 us; the launch traced here: 437 us
  waiting for transfers between devices  383 us (87%)
  local copies, waits for them, and re-layouts  18.5 us (4%)
  matrix products  17.4 us (4%)
  between operations  13.9 us (3%)
    psum x1, waiting for transfers between devices, per_device(): diagonal = lax.psum(diagonal, axis)  180 us
    all_gather x1, waiting for transfers between devices, per_device(): everything = lax.all_gather(masked, ('row', 'col'), axis=1, tiled=True)  127 us
    psum x1, waiting for transfers between devices, per_device(): whole = lax.psum(weighted, 'pole')  51.1 us
    reduce_scatter x1, waiting for transfers between devices, per_device(): density = lax.psum_scatter(whole, 'col', scatter_dimension=0, tiled=True)  24.3 us
    dot_general x4, matrix products, pair_product(): jnp.einsum('ika,kbi->kab', left, right, precision=lax.Precision.HIGHEST)  8.91 us
  transfers between devices with their start and end apart: 4, of which 4 were waited for; matrix products, arithmetic and copies ran while one was open for 5% of the time, Pallas kernels for 0%

profile of v1, /device:TPU:2, one launch (start us, length us, event | category | flops | bytes accessed | tf_op | source)
XLA Modules:
  0.0 437.3 jit_solution(10545760611642574836)
XLA Ops:
  7.9 0.7 fusion.25
  8.6 1.7 bitcast_select_fusion
  10.4 1.4 fusion.27
  11.7 3.8 fusion.26
  15.5 127.3 %all-gather.2.cloned.1.call-done = bf16[2,8192,512]{2,1,0:T(8,128)(2,1)} async-done(((bf16[2,128,512]{2,1,0:T(8,128)(2,1)}), bf16[2,8192,512]{2,1,0:T(8,128)(2,1)}) %all-gather.2.cloned.1.call-update) | async-done | bytes 16777232 | tf_op jit(solution)/shard_map/all_gather | solution.py:29
  142.8 1.7 constant_dynamic-slice_fusion.3
  144.6 1.3 fusion
  145.9 1.3 fusion.2
  147.5 1.3 fusion.12
  148.8 4.6 %multiply_subtract_fusion = (f32[512,1024]{1,0:T(8,128)}, f32[512,1024]{1,0:T(8,128)}) fusion(f32[512,1024]{1,0:T(8,128)S(1)} %fusion.12, f32[]{:T(128)} %bitcast.8, f32[]{:T(128)} %bitcast, f32[512,1024]{1,0:T(8,128)S(1)} %fusion, bf16[1024,512]{1,0:T(8,128)(2,1)S(1)} %bitcast.66, bf16[128,8,8,128]{3,2,1,0:T(8,128)(2,1)S(1)} %bitcast.64), kind=kOutput, calls=%fused_computation.8 | convolution fusion | flops 1076363264 | bytes 11534344 | tf_op jit(solution)/shard_map/jk,ij->ki/dot_general | solution.py:8
  153.5 0.9 copy-done.3
  154.4 1.3 subtract_multiply_fusion
  155.7 3.0 constant_dynamic-slice_fusion.2
  158.7 1.5 copy.9
  160.2 2.3 copy.8
  162.5 3.3 fusion.29
  165.8 1.2 fusion.28
  167.4 1.9 fusion.20
  169.2 2.5 fusion.19
  171.8 24.3 %reduce-scatter.2.cloned.1.call-done = f32[64,1024]{1,0:T(8,128)} async-done(((f32[512,1024]{1,0:T(8,128)}), f32[64,1024]{1,0:T(8,128)}) %reduce-scatter.2.cloned.1.call-update) | async-done | bytes 262160 | tf_op jit(solution)/shard_map/reduce_scatter | solution.py:44
  196.1 51.1 %all-reduce.6.cloned.1.call-done = (f32[64,1024]{1,0:T(8,128)}, f32[512,128]{1,0:T(8,128)}) async-done(((f32[64,1024]{1,0:T(8,128)}, f32[512,128]{1,0:T(8,128)}), (f32[64,1024]{1,0:T(8,128)}, f32[512,128]{1,0:T(8,128)})) %all-reduce.6.cloned.1.call-update) | async-done | bytes 524304 | tf_op jit(solution)/shard_map/psum | solution.py:43
  247.2 180.2 %all-reduce.4.cloned.1.call-done = f32[512,128]{1,0:T(8,128)} async-done(((f32[512,128]{1,0:T(8,128)}), f32[512,128]{1,0:T(8,128)}) %all-reduce.4.cloned.1.call-update) | async-done | bytes 262160 | tf_op jit(solution)/shard_map/psum | solution.py:58
  427.4 1.7 copy.37
  429.1 1.7 copy.38
  (16 shorter events, 1.5 us)
Async XLA Ops:
  7.2 135.7 %all-gather.2.cloned.1.call-start = ((), (), s32[]{:S(2)}) async-start(), calls=%async_computation.1 | async-start | bytes 17039360 | tf_op jit(solution)/shard_map/all_gather | solution.py:29
  10.3 185.7 %reduce-scatter.2.cloned.1.call-start = ((), (), s32[]{:S(2)}) async-start(), calls=%async_computation.3 | async-start | bytes 2359296 | tf_op jit(solution)/shard_map/reduce_scatter | solution.py:44
  145.9 1.6 copy-start.2
  153.4 0.9 copy-start.3
  153.4 93.8 %all-reduce.6.cloned.1.call-start = ((), (), s32[]{:S(2)}) async-start(), calls=%async_computation.4 | async-start | bytes 1048576 | tf_op jit(solution)/shard_map/psum | solution.py:43
  162.5 3.4 copy-start.1
  165.8 1.6 copy-start
  196.1 231.3 %all-reduce.4.cloned.1.call-start = ((), (), s32[]{:S(2)}) async-start(), calls=%async_computation.2 | async-start | bytes 524288 | tf_op jit(solution)/shard_map/psum | solution.py:58
Sparse Core Ops, SparseCore 0:
  10.4 132.3 all-gather.1
  153.6 42.4 reduce-scatter.1
  199.0 48.1 all-reduce.5
  250.5 176.7 all-reduce.3

commit v2 on v0

--- a/solution.py
+++ b/solution.py
@@ -1,7 +1,20 @@
+import functools
 import jax
 import jax.numpy as jnp
 from jax import lax
 from jax.sharding import PartitionSpec as P
+
+
+def _find_digits(u, pos_dim):
+    return jnp.concatenate(
+        lax.all_to_all(
+            jnp.stack([u for _ in range(lax.axis_size(("row", "col")))], 0), ("row", "col"), 0, 0
+        ),
+        axis=pos_dim,
+    )
+
+
+wait_zones = functools.partial(_find_digits, pos_dim=1)
 
 
 def contract(left, right):
@@ -26,7 +39,7 @@
     masked = jnp.where(
         (column_ok & block_ok)[None, None, :], l_panel[0], jnp.zeros((), jnp.bfloat16)
     )
-    everything = lax.all_gather(masked, ("row", "col"), axis=1, tiled=True)
+    everything = wait_zones(masked)
     own_rows = lax.dynamic_slice_in_dim(
         everything, row_index * col_count * slot_width, col_count * slot_width, 1
     )

time: 515 us -> 746 us (1.45)
  waiting for transfers between devices: 460 us -> 665 us
  local copies, waits for them, and re-layouts: 18.5 us -> 32 us
  starting transfers between devices: 0.16 us -> 12.6 us
    all_to_all x0 -> x1, waiting for transfers between devices: none -> 359 us  [_find_digits(): lax.all_to_all(jnp.stack([u for _ in range(lax.axis_size(('row', 'col')))...]
    all_gather x1 -> x0, waiting for transfers between devices: 127 us -> none  [per_device(): everything = lax.all_gather(masked, ('row', 'col'), axis=1, tiled=True)]
    psum x1, waiting for transfers between devices: 260 us -> 227 us  [per_device(): lax.psum(local_term.reshape(total_cols, slot_width), ('pole', 'row', 'col'))]
    all_to_all x0 -> x1, starting transfers between devices: none -> 12.3 us  [_find_digits(): lax.all_to_all(jnp.stack([u for _ in range(lax.axis_size(('row', 'col')))...]
    all_to_all x0 -> x1, local copies, waits for them, and re-layouts: none -> 8.48 us  [_find_digits(): lax.all_to_all(jnp.stack([u for _ in range(lax.axis_size(('row', 'col')))...]
  transfers between devices with their start and end apart: 4 -> 4, of which waited for: 4 -> 4; matrix products, arithmetic and copies ran while one was open for 4% -> 3% of each run, Pallas kernels for 0% -> 0%
where the time goes in v2:
time: 746 us; the launch traced here: 745 us
  waiting for transfers between devices  665 us (89%)
  local copies, waits for them, and re-layouts  32 us (4%)
  matrix products  16.7 us (2%)
  between operations  15.6 us (2%)
  starting transfers between devices  12.6 us (2%)
    all_to_all x1, waiting for transfers between devices, _find_digits(): lax.all_to_all(jnp.stack([u for _ in range(lax.axis_size(('row', 'col')))...  359 us
    psum x1, waiting for transfers between devices, per_device(): lax.psum(local_term.reshape(total_cols, slot_width), ('pole', 'row', 'col'))  227 us
    psum x1, waiting for transfers between devices, per_device(): whole = lax.psum(weighted, 'pole')  47.8 us
    reduce_scatter x1, waiting for transfers between devices, per_device(): density = lax.psum_scatter(whole, 'col', scatter_dimension=0, tiled=True)  31 us
  transfers between devices with their start and end apart: 4, of which 4 were waited for; matrix products, arithmetic and copies ran while one was open for 3% of the time, Pallas kernels for 0%

profile of v2, /device:TPU:2, one launch (start us, length us, event | category | flops | bytes accessed | tf_op | source)
XLA Modules:
  0.0 745.4 jit_solution(6149802220030964391)
XLA Ops:
  9.4 1.0 select_bitcast_fusion
  10.4 6.0 stack.5
  16.3 12.3 %all-to-all-start = ((bf16[64,2,128,512]{3,2,1,0:T(8,128)(2,1)}), bf16[64,2,128,512]{3,2,1,0:T(8,128)(2,1)}, u32[]{:S(2)}, u32[]{:S(2)}) async-start(bf16[64,2,128,512]{3,2,1,0:T(8,128)(2,1)} %stack.5), calls=%async_computation | async-start | bytes 33554432 | tf_op jit(solution)/shard_map/all_to_all | solution.py:10
  29.3 3.8 fusion.26
  33.1 358.7 %all-to-all-done = bf16[64,2,128,512]{3,2,1,0:T(8,128)(2,1)} async-done(((bf16[64,2,128,512]{3,2,1,0:T(8,128)(2,1)}), bf16[64,2,128,512]{3,2,1,0:T(8,128)(2,1)}, u32[]{:S(2)}, u32[]{:S(2)}) %all-to-all-start) | async-done | bytes 16777248 | tf_op jit(solution)/shard_map/all_to_all | solution.py:10
  391.8 8.5 %copy.11 = bf16[64,2,128,512]{3,2,0,1:T(8,128)(2,1)S(1)} copy(bf16[64,2,128,512]{3,2,1,0:T(8,128)(2,1)} %all-to-all-done) | data formatting | bytes 33554432 | tf_op jit(solution)/shard_map/all_to_all | solution.py:10
  400.6 1.3 fusion.2
  401.9 1.3 fusion
  403.2 3.5 copy-done
  406.6 1.3 fusion.12
  408.0 4.7 multiply_subtract_fusion
  413.6 1.3 subtract_multiply_fusion
  414.9 2.6 constant_dynamic-slice_fusion.2
  417.6 1.3 copy.14
  418.9 1.5 copy.15
  420.4 2.5 fusion.28
  423.0 1.2 fusion.29
  424.1 1.9 fusion.20
  426.0 2.5 fusion.19
  428.6 31.0 %reduce-scatter.2.cloned.1.call-done = f32[64,1024]{1,0:T(8,128)} async-done(((f32[512,1024]{1,0:T(8,128)}), f32[64,1024]{1,0:T(8,128)}) %reduce-scatter.2.cloned.1.call-update) | async-done | bytes 262160 | tf_op jit(solution)/shard_map/reduce_scatter | solution.py:57
  459.7 227.1 %all-reduce.3.cloned.1.call-done = f32[512,128]{1,0:T(8,128)} async-done(((f32[512,128]{1,0:T(8,128)}), f32[512,128]{1,0:T(8,128)}) %all-reduce.3.cloned.1.call-update) | async-done | bytes 262160 | tf_op jit(solution)/shard_map/psum | solution.py:69
  686.8 47.8 %all-reduce.5.cloned.1.call-done = f32[64,1024]{1,0:T(8,128)} async-done(((f32[64,1024]{1,0:T(8,128)}), f32[64,1024]{1,0:T(8,128)}) %all-reduce.5.cloned.1.call-update) | async-done | bytes 262160 | tf_op jit(solution)/shard_map/psum | solution.py:56
  734.6 1.7 copy.42
  736.3 1.7 copy.43
  (21 shorter events, 3.2 us)
Async XLA Ops:
  16.3 12.4 %copy-start.5 = (f32[1,2]{1,0:T(1,128)S(1)}, f32[1,2]{1,0:T(1,128)}, u32[]{:S(2)}) copy-start(f32[1,2]{1,0:T(1,128)} %param.11) | copy-start | bytes 28
  16.3 375.5 %all-to-all-start = ((bf16[64,2,128,512]{3,2,1,0:T(8,128)(2,1)}), bf16[64,2,128,512]{3,2,1,0:T(8,128)(2,1)}, u32[]{:S(2)}, u32[]{:S(2)}) async-start(bf16[64,2,128,512]{3,2,1,0:T(8,128)(2,1)} %stack.5), calls=%async_computation | async-start | bytes 33554432 | tf_op jit(solution)/shard_map/all_to_all | solution.py:10
  28.7 431.0 %reduce-scatter.2.cloned.1.call-start = ((), (), s32[]{:S(2)}) async-start(), calls=%async_computation.3 | async-start | bytes 2359296 | tf_op jit(solution)/shard_map/reduce_scatter | solution.py:57
  400.3 6.3 copy-start
  401.9 4.8 copy-start.3
  412.6 0.9 copy-start.4
  412.6 274.1 %all-reduce.3.cloned.1.call-start = ((), (), s32[]{:S(2)}) async-start(), calls=%async_computation.2 | async-start | bytes 524288 | tf_op jit(solution)/shard_map/psum | solution.py:69
  420.4 2.6 copy-start.1
  420.4 2.6 copy-start.2
  428.6 306.0 %all-reduce.5.cloned.1.call-start = ((), (), s32[]{:S(2)}) async-start(), calls=%async_computation.4 | async-start | bytes 524288 | tf_op jit(solution)/shard_map/psum | solution.py:56
Sparse Core Ops, SparseCore 0:
  412.8 46.8 reduce-scatter.1
Sparse Core Ops, SparseCore 1:
  428.7 258.1 all-reduce.2
  689.0 45.6 all-reduce.4
